TPU v7x, 32 devices: a whole 2x2x4 slice. The times are simulated.
32 devices in a mesh: cls: 8 (over y, x, core), batch: 4 (over z).
Axes of the slice: x: 2, y: 2, z: 4, core: 2. Of those that a mesh axis runs over, the one named last changes fastest.
Arguments:
- features: bfloat16 [4096, 1024], P('batch'), may hold values from -6 to 6
- head_weight: bfloat16 [1024, 1024], P('cls'), may hold values from -0.1875 to 0.1875
- inliers: bfloat16 [8192, 1024], P('cls'), may hold values from -2.5 to 2.5
- outliers: bfloat16 [8192, 1024], P('cls'), may hold values from -2.5 to 2.5
- inlier_counts: int32 [8192], P('cls'), may hold values from 1 to 9
- outlier_counts: int32 [8192], P('cls'), may hold values from 1 to 9
- labels: int32 [4096], P('batch'), may hold values from 0 to 1
Outputs:
- energy: float32 [4096], P('batch')
- head_grad: float32 [1024, 1024], P('cls')
All inputs are finite; a program needn't handle non-finite values.
Results may differ from a plain program's by a relative error of at most 0.0076.
The roundings to bfloat16 on the way count: a program that leaves them out, or rounds other values in their place, can miss the bound.
Values may be sent and summed in bfloat16 or wider, within the bound.
No kernel may reach another device: no remote copies, remote signals or barrier semaphores. Data moves between devices by JAX's collectives and lax.ppermute only.
A program may use at most 64 MiB of HBM per device.

v0:
```python
import jax
import jax.numpy as jnp
from jax import lax
from jax.sharding import PartitionSpec as P

beta = 2.0


def score_rows(queries, patterns, counts):
    log_counts = jnp.log(counts.astype(jnp.float32))
    return (
        beta * jnp.dot(queries, patterns.T, preferred_element_type=jnp.float32)
        + log_counts[None, :]
    )


def split_parts(values):
    high_part = values.astype(jnp.bfloat16)
    low_part = (values - high_part.astype(jnp.float32)).astype(jnp.bfloat16)
    return (high_part, low_part)


def outer_rows(columns, high_part, low_part):
    first = jnp.einsum("qf,qd->fd", columns, high_part, preferred_element_type=jnp.float32)
    return first + jnp.einsum("qf,qd->fd", columns, low_part, preferred_element_type=jnp.float32)


def body(features, head_weight, inliers, outliers, inlier_counts, outlier_counts, labels):
    columns = features
    queries = jnp.dot(
        columns,
        lax.all_gather(head_weight, "cls", axis=0, tiled=True),
        preferred_element_type=jnp.float32,
    ).astype(jnp.bfloat16)
    in_scores = score_rows(queries, inliers, inlier_counts)
    out_scores = score_rows(queries, outliers, outlier_counts)
    in_top, out_top = lax.pmax((jnp.max(in_scores, axis=1), jnp.max(out_scores, axis=1)), "cls")
    in_expon = jnp.exp(in_scores - in_top[:, None])
    out_expon = jnp.exp(out_scores - out_top[:, None])
    in_total, out_total = lax.psum((jnp.sum(in_expon, axis=1), jnp.sum(out_expon, axis=1)), "cls")
    in_sum = jnp.dot(in_expon.astype(jnp.bfloat16), inliers, preferred_element_type=jnp.float32)
    out_sum = jnp.dot(out_expon.astype(jnp.bfloat16), outliers, preferred_element_type=jnp.float32)
    energy = (in_top + jnp.log(in_total) - (out_top + jnp.log(out_total))) / beta
    label_sign = 2.0 * labels.astype(jnp.float32) - 1.0
    slope_term = -label_sign * jax.nn.sigmoid(-label_sign * energy)
    query_grad = slope_term[:, None] * (in_sum / in_total[:, None] - out_sum / out_total[:, None])
    grad_high, grad_low = split_parts(query_grad)
    columns = features
    partial_value = lax.psum_scatter(
        outer_rows(columns, grad_high, grad_low), "cls", scatter_dimension=0, tiled=True
    )
    head_grad = lax.psum(partial_value, "batch")
    return (energy, head_grad)


def solution(mesh):
    placed = (
        P("batch", None),
        P("cls", None),
        P("cls", None),
        P("cls", None),
        P("cls"),
        P("cls"),
        P("batch"),
    )
    return jax.shard_map(
        body, mesh=mesh, in_specs=placed, out_specs=(P("batch"), P("cls", None)), check_vma=False
    )
```

profile of v0, /device:TPU:0, one launch (start us, length us, event | category | flops | bytes accessed | tf_op | source)
XLA Modules:
  0.0 203.2 jit_solution(14456666442789482762)
XLA Ops:
  7.2 0.0 copy-start
  7.2 0.0 all-gather.2.cloned.1.call-start
  7.2 0.7 all-gather.2.cloned.1.call-update
  7.9 0.0 reduce-scatter.2.cloned.1.call-start
  8.0 0.7 convert_log_fusion.1
  8.7 0.7 convert_log_fusion
  9.3 31.1 %all-gather.2.cloned.1.call-done = bf16[1024,1024]{1,0:T(8,128)(2,1)} async-done(((bf16[128,1024]{1,0:T(8,128)(2,1)}), bf16[1024,1024]{1,0:T(8,128)(2,1)}) %all-gather.2.cloned.1.call-update) | async-done | bytes 2097168 | tf_op jit(solution)/shard_map/all_gather | solution.py:32
  40.4 0.0 copy-done
  40.4 4.1 %convolution_convert_fusion = bf16[1024,1024]{1,0:T(8,128)(2,1)S(1)} fusion(bf16[1024,1024]{1,0:T(8,128)(2,1)S(1)} %copy-done, bf16[1024,1024]{1,0:T(8,128)(2,1)} %all-gather.2.cloned.1.call-done), kind=kOutput, calls=%fused_computation.22 | convolution fusion | flops 2148532224 | bytes 6291456 | tf_op jit(solution)/shard_map/dot_general | solution.py:30
  44.5 0.0 copy-done.4
  44.5 0.0 copy-start.5
  44.5 4.3 %fusion.1 = (f32[1024]{0:T(1024)S(1)}, f32[1024,1024]{0,1:T(8,128)}) fusion(f32[1024]{0:T(1024)S(1)} %convert_log_fusion, bf16[1024,1024]{1,0:T(8,128)(2,1)S(1)} %convolution_convert_fusion, bf16[1024,1024]{1,0:T(8,128)(2,1)S(1)} %copy-done.4), kind=kOutput, calls=%fused_computation.8 | convolution fusion | flops 2150628352 | bytes 8396800 | tf_op jit(solution)/shard_map/dot_general | solution.py:12
  48.8 0.0 copy-done.5
  48.8 4.3 %fusion = (f32[1024]{0:T(1024)S(1)}, f32[1024,1024]{0,1:T(8,128)}) fusion(f32[1024]{0:T(1024)S(1)} %convert_log_fusion.1, bf16[1024,1024]{1,0:T(8,128)(2,1)S(1)} %convolution_convert_fusion, bf16[1024,1024]{1,0:T(8,128)(2,1)S(1)} %copy-done.5), kind=kOutput, calls=%fused_computation.7 | convolution fusion | flops 2150628352 | bytes 8396800 | tf_op jit(solution)/shard_map/dot_general | solution.py:12
  53.2 13.3 %all-reduce.1 = (f32[1024]{0:T(1024)S(1)}, f32[1024]{0:T(1024)S(1)}) all-reduce(f32[1024]{0:T(1024)S(1)} %get-tuple-element.10, f32[1024]{0:T(1024)S(1)} %get-tuple-element.12), channel_id=1, replica_groups=mesh['cls'=8,'batch'=4] {'cls'}, use_global_device_ids=true, to_apply=%region_5.0 | all-reduce | flops 2048 | bytes 16384 | tf_op jit(solution)/shard_map/pmax | solution.py:37
  66.5 0.0 copy-start.1
  66.5 0.0 copy-start.2
  66.5 7.5 %fusion.6 = f32[1024,1024]{1,0:T(8,128)} fusion(bf16[1024,1024]{1,0:T(8,128)(2,1)} %param.10, f32[1024,1024]{0,1:T(8,128)} %get-tuple-element.11, f32[1024]{0:T(1024)S(1)} %get-tuple-element.6, f32[1024]{0:T(1024)S(1)} %convert_log_fusion), kind=kOutput, calls=%fused_computation.13 | convolution fusion | flops 2151677952 | bytes 10493952 | tf_op jit(solution)/shard_map/dot_general | solution.py:42
  74.0 0.0 copy-done.1
  74.0 0.0 copy-done.2
  74.0 1.9 fusion.3
  75.9 12.2 %all-reduce = (f32[1024]{0:T(1024)S(1)}, f32[1024]{0:T(1024)S(1)}) all-reduce(f32[1024]{0:T(1024)S(1)} %get-tuple-element.15, f32[1024]{0:T(1024)S(1)} %get-tuple-element.14), channel_id=1, replica_groups=mesh['cls'=8,'batch'=4] {'cls'}, use_global_device_ids=true, to_apply=%region_7.0 | all-reduce | flops 2048 | bytes 16384 | tf_op jit(solution)/shard_map/psum | solution.py:40
  88.2 0.6 divide_multiply_fusion
  88.8 6.9 %subtract_multiply_fusion = f32[1024,1024]{1,0:T(8,128)S(1)} fusion(f32[1024,1024]{1,0:T(8,128)} %fusion.6, f32[1024]{0:T(1024)S(1)} %get-tuple-element.4, f32[1024]{0:T(1024)S(1)} %get-tuple-element.5, f32[1024]{0:T(1024)S(1)} %get-tuple-element.8, bf16[1024,1024]{1,0:T(8,128)(2,1)} %param.9, f32[1024,1024]{0,1:T(8,128)} %get-tuple-element.13, ...), kind=kOutput, calls=%fused_computation.2 | convolution fusion | flops 2155872256 | bytes 14700544 | tf_op jit(solution)/shard_map/dot_general | solution.py:41
  95.7 2.4 %fusion.20 = f32[1024,1024]{1,0:T(8,128)S(1)} fusion(bf16[1024,1024]{1,0:T(8,128)(2,1)S(1)} %copy-done, f32[1024,1024]{1,0:T(8,128)S(1)} %subtract_multiply_fusion), kind=kOutput, calls=%fused_computation.24 | convolution fusion | flops 2148532224 | bytes 10485760 | tf_op jit(solution)/shard_map/qf,qd->fd/dot_general | solution.py:24
  98.1 4.3 %add_bitcast_fusion = f32[1024,1024]{0,1:T(8,128)} fusion(f32[1024,1024]{1,0:T(8,128)S(1)} %fusion.20, bf16[1024,1024]{1,0:T(8,128)(2,1)S(1)} %copy-done, f32[1024,1024]{1,0:T(8,128)S(1)} %subtract_multiply_fusion), kind=kOutput, calls=%fused_computation | convolution fusion | flops 2152726528 | bytes 14680064 | tf_op jit(solution)/shard_map/qf,qd->fd/dot_general | solution.py:25
  102.4 0.0 reduce-scatter.2.cloned.1.call-update
  102.4 0.0 all-reduce.4.cloned.1.call-start
  102.4 51.3 %reduce-scatter.2.cloned.1.call-done = f32[128,1024]{0,1:T(8,128)} async-done(((f32[1024,1024]{0,1:T(8,128)}), f32[128,1024]{0,1:T(8,128)}) %reduce-scatter.2.cloned.1.call-update) | async-done | bytes 524304 | tf_op jit(solution)/shard_map/reduce_scatter | solution.py:49
  153.7 0.0 all-reduce.4.cloned.1.call-update
  153.7 40.9 %all-reduce.4.cloned.1.call-done = f32[128,1024]{0,1:T(8,128)} async-done(((f32[128,1024]{0,1:T(8,128)}), f32[128,1024]{0,1:T(8,128)}) %all-reduce.4.cloned.1.call-update) | async-done | bytes 524304 | tf_op jit(solution)/shard_map/psum | solution.py:52
  194.7 2.0 %copy.9 = f32[128,1024]{1,0:T(8,128)} copy(f32[128,1024]{0,1:T(8,128)} %all-reduce.4.cloned.1.call-done) | data formatting | bytes 1048576
  (3 shorter events, 0.0 us)
Async XLA Ops:
  7.2 33.2 %copy-start = (bf16[1024,1024]{1,0:T(8,128)(2,1)S(1)}, bf16[1024,1024]{1,0:T(8,128)(2,1)}, u32[]{:S(2)}) copy-start(bf16[1024,1024]{1,0:T(8,128)(2,1)} %param.7) | copy-start | bytes 6291460
  7.2 33.2 %all-gather.2.cloned.1.call-start = ((), (), s32[]{:S(2)}) async-start(), calls=%async_computation.1 | async-start | bytes 2359296 | tf_op jit(solution)/shard_map/all_gather | solution.py:32
  7.9 145.8 %reduce-scatter.2.cloned.1.call-start = ((), (), s32[]{:S(2)}) async-start(), calls=%async_computation.2 | async-start | bytes 4718592 | tf_op jit(solution)/shard_map/reduce_scatter | solution.py:49
  40.4 4.1 %copy-start.4 = (bf16[1024,1024]{1,0:T(8,128)(2,1)S(1)}, bf16[1024,1024]{1,0:T(8,128)(2,1)}, u32[]{:S(2)}) copy-start(bf16[1024,1024]{1,0:T(8,128)(2,1)} %param.10) | copy-start | bytes 6291460
  44.5 4.3 %copy-start.5 = (bf16[1024,1024]{1,0:T(8,128)(2,1)S(1)}, bf16[1024,1024]{1,0:T(8,128)(2,1)}, u32[]{:S(2)}) copy-start(bf16[1024,1024]{1,0:T(8,128)(2,1)} %param.9) | copy-start | bytes 6291460
  66.5 7.5 %copy-start.1 = (f32[1024,1024]{0,1:T(8,128)S(1)}, f32[1024,1024]{0,1:T(8,128)}, u32[]{:S(2)}) copy-start(f32[1024,1024]{0,1:T(8,128)} %get-tuple-element.13) | copy-start | bytes 12582916
  66.5 7.5 %copy-start.2 = (f32[1024,1024]{0,1:T(8,128)S(1)}, f32[1024,1024]{0,1:T(8,128)}, u32[]{:S(2)}) copy-start(f32[1024,1024]{0,1:T(8,128)} %get-tuple-element.11) | copy-start | bytes 12582916
  74.0 14.2 %copy-start.3 = (s32[1024]{0:T(1024)S(1)}, s32[1024]{0:T(1024)}, u32[]{:S(2)}) copy-start(s32[1024]{0:T(1024)} %param.13) | copy-start | bytes 12292
  102.4 92.3 %all-reduce.4.cloned.1.call-start = ((), (), s32[]{:S(2)}) async-start(), calls=%async_computation.3 | async-start | bytes 1048576 | tf_op jit(solution)/shard_map/psum | solution.py:52
Sparse Core Ops, SparseCore 0:
  9.9 30.4 all-gather.1
  102.5 51.1 reduce-scatter.1
  156.1 38.5 all-reduce.3
where the time goes:
time: 204 us; the launch traced here: 203 us
  waiting for transfers between devices  124 us (61%)
  matrix products  33.8 us (17%)
  blocking collectives  25.5 us (12%)
  between operations  13.8 us (7%)
  other arithmetic  3.94 us (2%)
  local copies, waits for them, and re-layouts  2.07 us (1%)
    reduce_scatter x1, waiting for transfers between devices, body(): lax.psum_scatter(outer_rows(columns, grad_high, grad_low), 'cls', scatter...  51.3 us
    psum x1, waiting for transfers between devices, body(): head_grad = lax.psum(partial_value, 'batch')  40.9 us
    all_gather x1, waiting for transfers between devices, body(): lax.all_gather(head_weight, 'cls', axis=0, tiled=True)  31.1 us
    pmax x1, blocking collectives, body(): lax.pmax((jnp.max(in_scores, axis=1), jnp.max(out_scores, axis=1)), 'cls')  13.3 us
    psum x1, blocking collectives, body(): lax.psum((jnp.sum(in_expon, axis=1), jnp.sum(out_expon, axis=1)), 'cls')  12.2 us
    dot_general x2, matrix products, score_rows(): jnp.dot(queries, patterns.T, preferred_element_type=jnp.float32)  8.65 us
    dot_general x1, matrix products, body(): jnp.dot(out_expon.astype(jnp.bfloat16), outliers, preferred_element_type=...  7.48 us
    dot_general x1, matrix products, body(): jnp.dot(in_expon.astype(jnp.bfloat16), inliers, preferred_element_type=jn...  6.85 us
  transfers between devices with their start and end apart: 3, of which 3 were waited for; matrix products, arithmetic and copies ran while one was open for 1% of the time, Pallas kernels for 0%

commit v1 on v0

--- a/solution.py
+++ b/solution.py
@@ -4,6 +4,18 @@
 from jax.sharding import PartitionSpec as P
 
 beta = 2.0
+
+
+def collect(x, axis, dim):
+    ways, here, step = (lax.axis_size(axis), lax.axis_index(axis), x.shape[dim])
+    line, have = (x, 1)
+    while have < ways:
+        line = jnp.concatenate(
+            [line, lax.ppermute(line, axis, [(d, (d - have) % ways) for d in range(ways)])],
+            axis=dim,
+        )
+        have = 2 * have
+    return jnp.roll(line, here * step, axis=dim)
 
 
 def score_rows(queries, patterns, counts):
@@ -28,9 +40,7 @@
 def body(features, head_weight, inliers, outliers, inlier_counts, outlier_counts, labels):
     columns = features
     queries = jnp.dot(
-        columns,
-        lax.all_gather(head_weight, "cls", axis=0, tiled=True),
-        preferred_element_type=jnp.float32,
+        columns, collect(head_weight, "cls", 0), preferred_element_type=jnp.float32
     ).astype(jnp.bfloat16)
     in_scores = score_rows(queries, inliers, inlier_counts)
     out_scores = score_rows(queries, outliers, outlier_counts)

time: 204 us -> 221 us (1.083)
  waiting for transfers between devices: 124 us -> 131 us
  starting transfers between devices: 0.12 us -> 4.75 us
  local copies, waits for them, and re-layouts: 2.07 us -> 5.76 us
  other arithmetic: 3.94 us -> 6.92 us
    ppermute x0 -> x3, waiting for transfers between devices: none -> 39.7 us  [collect(): lax.ppermute(line, axis, [(d, (d - have) % ways) for d in range(ways)])]
    all_gather x1 -> x0, waiting for transfers between devices: 31.1 us -> none  [body(): lax.all_gather(head_weight, 'cls', axis=0, tiled=True)]
    ppermute x0 -> x3, starting transfers between devices: none -> 4.67 us  [collect(): lax.ppermute(line, axis, [(d, (d - have) % ways) for d in range(ways)])]
    concatenate x0 -> x2, other arithmetic: none -> 2.99 us  [collect(): jnp.concatenate([line, lax.ppermute(line, axis, [(d, (d - have) % ways) f...]
    unnamed x13 -> x22, local copies, waits for them, and re-layouts: 2.07 us -> 4.47 us
  transfers between devices with their start and end apart: 3 -> 5, of which waited for: 3 -> 5; matrix products, arithmetic and copies ran while one was open for 1% -> 1% of each run, Pallas kernels for 0% -> 0%
where the time goes in v1:
time: 221 us
  waiting for transfers between devices  131 us (59%)
  matrix products  32.6 us (15%)
  blocking collectives  25.6 us (12%)
  between operations  14.2 us (6%)
  other arithmetic  6.92 us (3%)
  local copies, waits for them, and re-layouts  5.76 us (3%)
  starting transfers between devices  4.75 us (2%)
    reduce_scatter x1, waiting for transfers between devices, body(): lax.psum_scatter(outer_rows(columns, grad_high, grad_low), 'cls', scatter...  50.5 us
    psum x1, waiting for transfers between devices, body(): head_grad = lax.psum(partial_value, 'batch')  40.9 us
    ppermute x3, waiting for transfers between devices, collect(): lax.ppermute(line, axis, [(d, (d - have) % ways) for d in range(ways)])  39.7 us
    pmax x1, blocking collectives, body(): lax.pmax((jnp.max(in_scores, axis=1), jnp.max(out_scores, axis=1)), 'cls')  13.3 us
    psum x1, blocking collectives, body(): lax.psum((jnp.sum(in_expon, axis=1), jnp.sum(out_expon, axis=1)), 'cls')  12.3 us
    dot_general x2, matrix products, score_rows(): jnp.dot(queries, patterns.T, preferred_element_type=jnp.float32)  8.58 us
    dot_general x1, matrix products, body(): jnp.dot(out_expon.astype(jnp.bfloat16), outliers, preferred_element_type=...  7.49 us
    dot_general x1, matrix products, body(): jnp.dot(in_expon.astype(jnp.bfloat16), inliers, preferred_element_type=jn...  7.08 us
  transfers between devices with their start and end apart: 5, of which 5 were waited for; matrix products, arithmetic and copies ran while one was open for 1% of the time, Pallas kernels for 0%

profile of v1, /device:TPU:0, one launch (start us, length us, event | category | flops | bytes accessed | tf_op | source)
XLA Modules:
  0.0 221.1 jit_solution(3358176658697701278)
XLA Ops:
  7.2 0.0 copy-start
  7.2 0.0 reduce-scatter.2.cloned.1.call-start
  7.2 3.4 %collective-permute-start = (bf16[128,1024]{1,0:T(8,128)(2,1)}, bf16[128,1024]{1,0:T(8,128)(2,1)S(1)}, u32[]{:S(2)}, u32[]{:S(2)}) collective-permute-start(bf16[128,1024]{1,0:T(8,128)(2,1)} %param.8), channel_id=1, source_target_pairs={{0,28},{4,0},{8,4},{12,8},{16,12},{20,16},{24,20},{28,24},{1,29},{... | collective-permute-start | bytes 786440 | tf_op jit(solution)/shard_map/ppermute | solution.py:14
  10.7 4.2 %collective-permute-done = bf16[128,1024]{1,0:T(8,128)(2,1)S(1)} collective-permute-done((bf16[128,1024]{1,0:T(8,128)(2,1)}, bf16[128,1024]{1,0:T(8,128)(2,1)S(1)}, u32[]{:S(2)}, u32[]{:S(2)}) %collective-permute-start) | collective-permute-done | bytes 262176 | tf_op jit(solution)/shard_map/ppermute | solution.py:14
  14.9 1.0 pad_maximum_fusion.1
  15.8 0.6 collective-permute-start.1
  16.5 13.7 %collective-permute-done.1 = bf16[256,1024]{1,0:T(8,128)(2,1)S(1)} collective-permute-done((bf16[256,1024]{1,0:T(8,128)(2,1)S(1)}, bf16[256,1024]{1,0:T(8,128)(2,1)S(1)}, u32[]{:S(2)}, u32[]{:S(2)}) %collective-permute-start.1) | collective-permute-done | bytes 524320 | tf_op jit(solution)/shard_map/ppermute | solution.py:14
  30.1 2.0 pad_maximum_fusion
  32.1 0.6 collective-permute-start.2
  32.8 1.0 constant_dynamic-update-slice_fusion.7
  33.7 0.7 convert_log_fusion.1
  34.4 0.7 convert_log_fusion
  35.2 21.9 %collective-permute-done.2 = bf16[512,1024]{1,0:T(8,128)(2,1)} collective-permute-done((bf16[512,1024]{1,0:T(8,128)(2,1)}, bf16[512,1024]{1,0:T(8,128)(2,1)}, u32[]{:S(2)}, u32[]{:S(2)}) %collective-permute-start.2) | collective-permute-done | bytes 1048608 | tf_op jit(solution)/shard_map/ppermute | solution.py:14
  57.1 1.3 constant_dynamic-update-slice_fusion.4
  58.5 1.3 constant_dynamic-update-slice_fusion
  59.8 2.4 %fusion.21 = bf16[1024,1024]{1,0:T(8,128)(2,1)S(1)} fusion(bf16[1024,1024]{1,0:T(8,128)(2,1)S(1)} %copy-done, bf16[2048,1024]{1,0:T(8,128)(2,1)S(1)} %constant_dynamic-update-slice_fusion, s32[]{:T(128)S(6)} %select_n.14), kind=kOutput, calls=%fused_computation.24 | convolution fusion | flops 2148532224 | bytes 6291460 | tf_op jit(solution)/shard_map/dot_general | solution.py:42
  62.2 4.3 %fusion.1 = (f32[1024]{0:T(1024)S(1)}, f32[1024,1024]{0,1:T(8,128)}) fusion(f32[1024]{0:T(1024)S(1)} %convert_log_fusion, bf16[1024,1024]{1,0:T(8,128)(2,1)S(1)} %copy-done.5, bf16[1024,1024]{1,0:T(8,128)(2,1)S(1)} %fusion.21), kind=kOutput, calls=%fused_computation.8 | convolution fusion | flops 2150628352 | bytes 8396800 | tf_op jit(solution)/shard_map/dot_general | solution.py:24
  66.5 4.3 %fusion = (f32[1024]{0:T(1024)S(1)}, f32[1024,1024]{0,1:T(8,128)}) fusion(f32[1024]{0:T(1024)S(1)} %convert_log_fusion.1, bf16[1024,1024]{1,0:T(8,128)(2,1)S(1)} %copy-done.6, bf16[1024,1024]{1,0:T(8,128)(2,1)S(1)} %fusion.21), kind=kOutput, calls=%fused_computation.7 | convolution fusion | flops 2150628352 | bytes 8396800 | tf_op jit(solution)/shard_map/dot_general | solution.py:24
  70.8 13.3 %all-reduce.1 = (f32[1024]{0:T(1024)S(1)}, f32[1024]{0:T(1024)S(1)}) all-reduce(f32[1024]{0:T(1024)S(1)} %get-tuple-element.10, f32[1024]{0:T(1024)S(1)} %get-tuple-element.12), channel_id=1, replica_groups=mesh['cls'=8,'batch'=4] {'cls'}, use_global_device_ids=true, to_apply=%region_5.6 | all-reduce | flops 2048 | bytes 16384 | tf_op jit(solution)/shard_map/pmax | solution.py:47
  84.2 7.5 %fusion.6 = f32[1024,1024]{1,0:T(8,128)} fusion(bf16[1024,1024]{1,0:T(8,128)(2,1)} %param.10, f32[1024,1024]{0,1:T(8,128)} %get-tuple-element.11, f32[1024]{0:T(1024)S(1)} %get-tuple-element.6, f32[1024]{0:T(1024)S(1)} %convert_log_fusion), kind=kOutput, calls=%fused_computation.13 | convolution fusion | flops 2151677952 | bytes 10493952 | tf_op jit(solution)/shard_map/dot_general | solution.py:52
  91.7 1.9 fusion.3
  93.6 12.3 %all-reduce = (f32[1024]{0:T(1024)S(1)}, f32[1024]{0:T(1024)S(1)}) all-reduce(f32[1024]{0:T(1024)S(1)} %get-tuple-element.15, f32[1024]{0:T(1024)S(1)} %get-tuple-element.14), channel_id=1, replica_groups=mesh['cls'=8,'batch'=4] {'cls'}, use_global_device_ids=true, to_apply=%region_7.8 | all-reduce | flops 2048 | bytes 16384 | tf_op jit(solution)/shard_map/psum | solution.py:50
  105.9 0.6 divide_multiply_fusion
  106.5 7.1 %subtract_multiply_fusion = f32[1024,1024]{1,0:T(8,128)S(1)} fusion(f32[1024,1024]{1,0:T(8,128)} %fusion.6, f32[1024]{0:T(1024)S(1)} %get-tuple-element.4, f32[1024]{0:T(1024)S(1)} %get-tuple-element.5, f32[1024]{0:T(1024)S(1)} %get-tuple-element.8, bf16[1024,1024]{1,0:T(8,128)(2,1)} %param.9, f32[1024,1024]{0,1:T(8,128)} %get-tuple-element.13, ...), kind=kOutput, calls=%fused_computation.2 | convolution fusion | flops 2155872256 | bytes 14700544 | tf_op jit(solution)/shard_map/dot_general | solution.py:51
  113.6 2.5 %fusion.25 = f32[1024,1024]{1,0:T(8,128)S(1)} fusion(bf16[1024,1024]{1,0:T(8,128)(2,1)S(1)} %copy-done, f32[1024,1024]{1,0:T(8,128)S(1)} %subtract_multiply_fusion), kind=kOutput, calls=%fused_computation.27 | convolution fusion | flops 2148532224 | bytes 10485760 | tf_op jit(solution)/shard_map/qf,qd->fd/dot_general | solution.py:36
  116.1 4.5 %add_bitcast_fusion = f32[1024,1024]{0,1:T(8,128)} fusion(f32[1024,1024]{1,0:T(8,128)S(1)} %fusion.25, bf16[1024,1024]{1,0:T(8,128)(2,1)S(1)} %copy-done, f32[1024,1024]{1,0:T(8,128)S(1)} %subtract_multiply_fusion), kind=kOutput, calls=%fused_computation | convolution fusion | flops 2152726528 | bytes 14680064 | tf_op jit(solution)/shard_map/qf,qd->fd/dot_general | solution.py:37
  120.6 0.0 reduce-scatter.2.cloned.1.call-update
  120.7 0.0 all-reduce.4.cloned.1.call-start
  120.7 50.5 %reduce-scatter.2.cloned.1.call-done = f32[128,1024]{0,1:T(8,128)} async-done(((f32[1024,1024]{0,1:T(8,128)}), f32[128,1024]{0,1:T(8,128)}) %reduce-scatter.2.cloned.1.call-update) | async-done | bytes 524304 | tf_op jit(solution)/shard_map/reduce_scatter | solution.py:59
  171.3 0.0 all-reduce.4.cloned.1.call-update
  171.3 40.9 %all-reduce.4.cloned.1.call-done = f32[128,1024]{0,1:T(8,128)} async-done(((f32[128,1024]{0,1:T(8,128)}), f32[128,1024]{0,1:T(8,128)}) %all-reduce.4.cloned.1.call-update) | async-done | bytes 524304 | tf_op jit(solution)/shard_map/psum | solution.py:62
  212.2 2.0 copy.9
  (18 shorter events, 0.2 us)
Async XLA Ops:
  7.2 52.6 %copy-start = (bf16[1024,1024]{1,0:T(8,128)(2,1)S(1)}, bf16[1024,1024]{1,0:T(8,128)(2,1)}, u32[]{:S(2)}) copy-start(bf16[1024,1024]{1,0:T(8,128)(2,1)} %param.7) | copy-start | bytes 6291460
  7.2 51.2 %copy-start.3 = (bf16[128,1024]{1,0:T(8,128)(2,1)S(1)}, bf16[128,1024]{1,0:T(8,128)(2,1)}, u32[]{:S(2)}) copy-start(bf16[128,1024]{1,0:T(8,128)(2,1)} %param.8) | copy-start | bytes 786436
  7.2 164.1 %reduce-scatter.2.cloned.1.call-start = ((), (), s32[]{:S(2)}) async-start(), calls=%async_computation.1 | async-start | bytes 4718592 | tf_op jit(solution)/shard_map/reduce_scatter | solution.py:59
  7.2 7.6 %collective-permute-start = (bf16[128,1024]{1,0:T(8,128)(2,1)}, bf16[128,1024]{1,0:T(8,128)(2,1)S(1)}, u32[]{:S(2)}, u32[]{:S(2)}) collective-permute-start(bf16[128,1024]{1,0:T(8,128)(2,1)} %param.8), channel_id=1, source_target_pairs={{0,28},{4,0},{8,4},{12,8},{16,12},{20,16},{24,20},{28,24},{1,29},{... | collective-permute-start | bytes 786440 | tf_op jit(solution)/shard_map/ppermute | solution.py:14
  15.8 14.3 %collective-permute-start.1 = (bf16[256,1024]{1,0:T(8,128)(2,1)S(1)}, bf16[256,1024]{1,0:T(8,128)(2,1)S(1)}, u32[]{:S(2)}, u32[]{:S(2)}) collective-permute-start(bf16[256,1024]{1,0:T(8,128)(2,1)S(1)} %pad_maximum_fusion.1), channel_id=1, source_target_pairs={{0,24},{4,28},{8,0},{12,4},{16,8},{20,12},{24,16},{28,20},{1,25},{... | collective-permute-start | bytes 1572872 | tf_op jit(solution)/shard_map/ppermute | solution.py:14
  32.1 24.9 %collective-permute-start.2 = (bf16[512,1024]{1,0:T(8,128)(2,1)}, bf16[512,1024]{1,0:T(8,128)(2,1)}, u32[]{:S(2)}, u32[]{:S(2)}) collective-permute-start(bf16[512,1024]{1,0:T(8,128)(2,1)} %pad_maximum_fusion), channel_id=1, source_target_pairs={{0,16},{4,20},{8,24},{12,28},{16,0},{20,4},{24,8},{28,12},{1,17},{... | collective-permute-start | bytes 3145736 | tf_op jit(solution)/shard_map/ppermute | solution.py:14
  59.8 2.4 %copy-start.5 = (bf16[1024,1024]{1,0:T(8,128)(2,1)S(1)}, bf16[1024,1024]{1,0:T(8,128)(2,1)}, u32[]{:S(2)}) copy-start(bf16[1024,1024]{1,0:T(8,128)(2,1)} %param.10) | copy-start | bytes 6291460
  62.2 4.3 %copy-start.6 = (bf16[1024,1024]{1,0:T(8,128)(2,1)S(1)}, bf16[1024,1024]{1,0:T(8,128)(2,1)}, u32[]{:S(2)}) copy-start(bf16[1024,1024]{1,0:T(8,128)(2,1)} %param.9) | copy-start | bytes 6291460
  84.1 7.5 %copy-start.1 = (f32[1024,1024]{0,1:T(8,128)S(1)}, f32[1024,1024]{0,1:T(8,128)}, u32[]{:S(2)}) copy-start(f32[1024,1024]{0,1:T(8,128)} %get-tuple-element.13) | copy-start | bytes 12582916
  84.2 7.5 %copy-start.2 = (f32[1024,1024]{0,1:T(8,128)S(1)}, f32[1024,1024]{0,1:T(8,128)}, u32[]{:S(2)}) copy-start(f32[1024,1024]{0,1:T(8,128)} %get-tuple-element.11) | copy-start | bytes 12582916
  91.7 14.3 %copy-start.4 = (s32[1024]{0:T(1024)S(1)}, s32[1024]{0:T(1024)}, u32[]{:S(2)}) copy-start(s32[1024]{0:T(1024)} %param.13) | copy-start | bytes 12292
  120.7 91.5 %all-reduce.4.cloned.1.call-start = ((), (), s32[]{:S(2)}) async-start(), calls=%async_computation.2 | async-start | bytes 1048576 | tf_op jit(solution)/shard_map/psum | solution.py:62
Sparse Core Ops, SparseCore 0:
  120.8 50.4 reduce-scatter.1
  173.6 38.5 all-reduce.3
